TPU v7x, 256 devices: a whole 4x4x8 slice. The times are simulated.
256 devices in a mesh: rows: 128 (over x, z, y), cols: 2 (over core).
Axes of the slice: x: 4, y: 4, z: 8, core: 2. Of those that a mesh axis runs over, the one named last changes fastest.
Arguments:
- embeddings: bfloat16 [262144, 384], P('rows')
- test_matrix: bfloat16 [262144, 64], P('rows'), may hold values from -6 to 6
- pair_list: int32 [1024, 2], P(('rows', 'cols')), may hold values from -1 to 255, as said below
Outputs:
- orthonormal_basis: float32 [262144, 64], P(('rows', 'cols'))
- upper_factor: float32 [64, 64], replicated
Inputs may be any that keep to these rules, and one draw needn't show every extreme that they name: `pair_list`: device (r, c) holds 4 entries. Its live entries come first: pairs (i, j) with r * 2 <= i < (r + 1) * 2 and i <= j < min((r + 3) * 2, 256); each pair appears at most once over all devices; its other entries are -1 in both places. The device with c = 0 holds at least one live pair, the two devices of one r hold at most 4 together, and device (0, 0) holds exactly 4.
All inputs are finite; a program needn't handle non-finite values.
Results may differ from a plain program's by a relative error of at most 0.0053.
Values may be sent and summed in bfloat16 or wider, within the bound.
No kernel may reach another device: no remote copies, remote signals or barrier semaphores. Data moves between devices by JAX's collectives and lax.ppermute only.
A program may use at most 64 MiB of HBM per device.

v0:
```python
import jax
import jax.numpy as jnp
from jax import lax
from jax.sharding import PartitionSpec as P

BLK = 1024
SHARPNESS = 6.0
EPSILON = 1e-06


def shifted(value, axis, steps):
    count = lax.axis_size(axis)
    initial, last = (max(0, -steps), min(count, count - steps))
    return lax.ppermute(value, axis, [(source, source + steps) for source in range(initial, last)])


def unit_rows(embeddings):
    widened = embeddings.astype(jnp.float32)
    inverse = lax.rsqrt(jnp.sum(widened * widened, axis=1, keepdims=True) + EPSILON)
    return (widened * inverse).astype(jnp.bfloat16)


def affinity(left_rows, right_rows):
    scores = lax.dot_general(
        left_rows, right_rows, (((1,), (1,)), ((), ())), preferred_element_type=jnp.float32
    )
    return jnp.exp(SHARPNESS * (scores - 1.0)).astype(jnp.bfloat16)


def mirror_product(affinity_tile, vectors):
    return lax.dot_general(
        affinity_tile, vectors, (((0,), (0,)), ((), ())), preferred_element_type=jnp.float32
    )


def block_at(stacked, index):
    return lax.dynamic_index_in_dim(stacked, index, 0, keepdims=False)


def add_block(stacked, index, term):
    return lax.dynamic_update_index_in_dim(stacked, block_at(stacked, index) + term, index, 0)


def count_live(pair_rows):
    return jnp.sum((pair_rows[:, 0] >= 0).astype(jnp.int32))


def orthonormal(sketch_rows, rows_total):
    gram_matrix = lax.dot_general(
        sketch_rows,
        sketch_rows,
        (((0,), (0,)), ((), ())),
        precision=lax.Precision.HIGHEST,
        preferred_element_type=jnp.float32,
    )
    gram_matrix = lax.psum(gram_matrix, ("rows", "cols")) / rows_total
    lower_factor = jnp.linalg.cholesky(gram_matrix)
    solved = lax.linalg.triangular_solve(
        lower_factor, sketch_rows, left_side=False, lower=True, transpose_a=True
    )
    return (solved, lower_factor.T)


def affinity_pass(window_units, own_vectors, my_pairs, base_block):
    blocks_dev = own_vectors.shape[0]
    ahead_vectors = [shifted(own_vectors, "rows", -offset) for offset in (1, 2)]
    window_vectors = jnp.concatenate([own_vectors] + ahead_vectors, axis=0)
    initial = jnp.zeros(window_vectors.shape, jnp.float32)

    def pair_step(slot_index, accumulated):
        entry = my_pairs[slot_index]
        first_block = entry[0] - base_block
        second_block = entry[1] - base_block
        affinity_tile = affinity(
            block_at(window_units, first_block), block_at(window_units, second_block)
        )
        forward = jnp.dot(
            affinity_tile,
            block_at(window_vectors, second_block),
            preferred_element_type=jnp.float32,
        )
        accumulated = add_block(accumulated, first_block, forward)
        mirrored = first_block != second_block

        def add_mirror(current):
            return add_block(
                current,
                second_block,
                mirror_product(affinity_tile, block_at(window_vectors, first_block)),
            )

        return lax.cond(mirrored, add_mirror, lambda unchanged: unchanged, accumulated)

    accumulated = lax.fori_loop(0, count_live(my_pairs), pair_step, initial)
    own_blocks = accumulated[:blocks_dev]
    for offset in (1, 2):
        own_blocks = own_blocks + shifted(
            accumulated[offset * blocks_dev : (offset + 1) * blocks_dev], "rows", offset
        )
    flattened = own_blocks.reshape(-1, own_blocks.shape[2])
    return lax.psum_scatter(flattened, "cols", scatter_dimension=0, tiled=True)


def local(embeddings, test_matrix, pair_list):
    rows_dev = embeddings.shape[0]
    blocks_dev = rows_dev // BLK
    columns = test_matrix.shape[1]
    base_block = lax.axis_index("rows") * blocks_dev
    rows_total = rows_dev * lax.axis_size("rows")
    normed = unit_rows(embeddings).reshape(blocks_dev, BLK, embeddings.shape[1])
    ahead_units = [shifted(normed, "rows", -offset) for offset in (1, 2)]
    window_units = jnp.concatenate([normed] + ahead_units, axis=0)
    sketch_rows = affinity_pass(
        window_units, test_matrix.reshape(blocks_dev, BLK, columns), pair_list, base_block
    )
    panel_rows, _ = orthonormal(sketch_rows, rows_total)
    panel_whole = lax.all_gather(panel_rows.astype(jnp.bfloat16), "cols", axis=0, tiled=True)
    image_rows = affinity_pass(
        window_units, panel_whole.reshape(blocks_dev, BLK, columns), pair_list, base_block
    )
    return orthonormal(image_rows, rows_total)


def solution(mesh):
    in_specs = (P("rows", None), P("rows", None), P(("rows", "cols"), None))
    out_specs = (P(("rows", "cols"), None), P())
    return jax.shard_map(local, mesh=mesh, in_specs=in_specs, out_specs=out_specs, check_vma=False)
```

profile of v0, /device:TPU:1, one launch (start us, length us, event | category | flops | bytes accessed | tf_op | source)
XLA Modules:
  0.0 547.8 jit_solution(13680197383918252103)
XLA Ops:
  7.2 1.9 fusion.32
  9.2 0.3 fusion.33
  9.5 1.3 collective-permute-start
  10.8 1.3 collective-permute-start.1
  12.4 1.3 collective-permute-start.2
  13.7 1.3 collective-permute-start.3
  15.0 0.6 fusion.44
  15.7 85.9 %collective-permute-done.2 = bf16[2,1024,64]{2,1,0:T(8,128)(2,1)S(1)} collective-permute-done((bf16[2,1024,64]{2,1,0:T(8,128)(2,1)S(1)}, bf16[2,1024,64]{2,1,0:T(8,128)(2,1)S(1)}, u32[]{:S(2)}, u32[]{:S(2)}) %collective-permute-start.2) | collective-permute-done | bytes 262176 | tf_op jit(solution)/shard_map/ppermute | solution.py:14
  101.6 1.5 pad_maximum_fusion.1
  103.1 3.8 pad_maximum_fusion
  106.9 1.3 broadcast.76.clone
  108.3 0.7 while.24
  108.9 1.3 fusion.48
  110.2 6.4 %collective-permute-start.4 = (f32[2,1024,64]{1,2,0:T(8,128)S(1)}, f32[2,1024,64]{1,2,0:T(8,128)S(1)}, u32[]{:S(2)}, u32[]{:S(2)}) collective-permute-start(f32[2,1024,64]{1,2,0:T(8,128)S(1)} %get-tuple-element.272), channel_id=1, source_target_pairs={{0,2},{2,4},{4,6},{6,8},{8,10},{10,12},{12,14},{14,16},{16,18},{18... | collective-permute-start | bytes 1572872 | tf_op jit(solution)/shard_map/ppermute | solution.py:14
  116.6 72.9 %collective-permute-start.5 = (f32[2,1024,64]{1,2,0:T(8,128)S(1)}, f32[2,1024,64]{1,2,0:T(8,128)S(1)}, u32[]{:S(2)}, u32[]{:S(2)}) collective-permute-start(f32[2,1024,64]{1,2,0:T(8,128)S(1)} %get-tuple-element.273), channel_id=1, source_target_pairs={{0,4},{2,6},{4,8},{6,10},{8,12},{10,14},{12,16},{14,18},{16,20},{1... | collective-permute-start | bytes 1572872 | tf_op jit(solution)/shard_map/ppermute | solution.py:14
  189.5 6.1 %collective-permute-done.5 = f32[2,1024,64]{1,2,0:T(8,128)S(1)} collective-permute-done((f32[2,1024,64]{1,2,0:T(8,128)S(1)}, f32[2,1024,64]{1,2,0:T(8,128)S(1)}, u32[]{:S(2)}, u32[]{:S(2)}) %collective-permute-start.5) | collective-permute-done | bytes 524320 | tf_op jit(solution)/shard_map/ppermute | solution.py:14
  195.6 1.1 add_bitcast_fusion.1
  196.8 0.9 copy.28
  197.7 36.3 %reduce-scatter.3.cloned.1.call-done = f32[1024,64]{0,1:T(8,128)} async-done(((f32[2048,64]{0,1:T(8,128)}), f32[1024,64]{0,1:T(8,128)}) %reduce-scatter.3.cloned.1.call-update) | async-done | bytes 262160 | tf_op jit(solution)/shard_map/reduce_scatter | solution.py:101
  234.0 1.4 fusion.49
  235.5 77.5 %psum.14 = f32[64,64]{0,1:T(8,128)S(1)} all-reduce(f32[64,64]{0,1:T(8,128)S(1)} %fusion.49), channel_id=1, replica_groups=mesh['rows'=128,'cols'=2] {'rows','cols'}, use_global_device_ids=true, to_apply=%region_7.8 | all-reduce | flops 4096 | bytes 32768 | tf_op jit(solution)/shard_map/psum | solution.py:56
  313.1 5.8 %cholesky.44 = f32[64,64]{1,0:T(8,128)S(1)} custom-call(f32[64,64]{1,0:T(8,128)S(1)} %fusion.39), custom_call_target="Cholesky" | custom-call | tf_op jit(solution)/shard_map/jit(cholesky)/cholesky | solution.py:57
  319.0 0.6 compare_reduce_fusion.1
  319.6 0.7 fusion.35
  320.3 4.9 custom-call.6
  325.2 1.4 fusion.34
  326.6 2.5 all_gather.3
  329.4 1.3 collective-permute-start.6
  330.7 1.3 collective-permute-start.7
  332.0 22.3 %collective-permute-done.6 = bf16[2,1024,64]{2,1,0:T(8,128)(2,1)S(1)} collective-permute-done((bf16[2,1024,64]{2,1,0:T(8,128)(2,1)S(1)}, bf16[2,1024,64]{2,1,0:T(8,128)(2,1)S(1)}, u32[]{:S(2)}, u32[]{:S(2)}) %collective-permute-start.6) | collective-permute-done | bytes 262176 | tf_op jit(solution)/shard_map/ppermute | solution.py:14
  354.2 1.5 pad_maximum_fusion.2
  355.8 1.3 broadcast.76
  357.1 0.7 while.25
  357.7 1.3 fusion.47
  359.1 3.7 collective-permute-start.8
  362.7 45.1 %collective-permute-start.9 = (f32[2,1024,64]{1,2,0:T(8,128)S(1)}, f32[2,1024,64]{1,2,0:T(8,128)S(1)}, u32[]{:S(2)}, u32[]{:S(2)}) collective-permute-start(f32[2,1024,64]{1,2,0:T(8,128)S(1)} %get-tuple-element.271), channel_id=1, source_target_pairs={{0,4},{2,6},{4,8},{6,10},{8,12},{10,14},{12,16},{14,18},{16,20},{1... | collective-permute-start | bytes 1572872 | tf_op jit(solution)/shard_map/ppermute | solution.py:14
  407.8 11.5 %collective-permute-done.9 = f32[2,1024,64]{1,2,0:T(8,128)S(1)} collective-permute-done((f32[2,1024,64]{1,2,0:T(8,128)S(1)}, f32[2,1024,64]{1,2,0:T(8,128)S(1)}, u32[]{:S(2)}, u32[]{:S(2)}) %collective-permute-start.9) | collective-permute-done | bytes 524320 | tf_op jit(solution)/shard_map/ppermute | solution.py:14
  419.3 1.1 add_bitcast_fusion
  420.4 0.8 copy.29
  421.3 25.8 %reduce-scatter.5.cloned.1.call-done = f32[1024,64]{0,1:T(8,128)} async-done(((f32[2048,64]{0,1:T(8,128)}), f32[1024,64]{0,1:T(8,128)}) %reduce-scatter.5.cloned.1.call-update) | async-done | bytes 262160 | tf_op jit(solution)/shard_map/reduce_scatter | solution.py:101
  447.1 1.4 fusion.50
  448.4 77.5 %psum.15 = f32[64,64]{0,1:T(8,128)S(1)} all-reduce(f32[64,64]{0,1:T(8,128)S(1)} %fusion.50), channel_id=1, replica_groups=mesh['rows'=128,'cols'=2] {'rows','cols'}, use_global_device_ids=true, to_apply=%region_15.18 | all-reduce | flops 4096 | bytes 32768 | tf_op jit(solution)/shard_map/psum | solution.py:56
  526.1 5.8 %cholesky.55 = f32[64,64]{1,0:T(8,128)S(1)} custom-call(f32[64,64]{1,0:T(8,128)S(1)} %fusion.37), custom_call_target="Cholesky" | custom-call | tf_op jit(solution)/shard_map/jit(cholesky)/cholesky | solution.py:57
  532.0 0.6 compare_reduce_fusion
  532.6 0.7 fusion.43
  533.3 4.9 custom-call.7
  538.2 0.7 copy.24
  538.9 2.1 convolution_bitcast_fusion.2
  (27 shorter events, 0.9 us)
Async XLA Ops:
  7.2 2.0 copy-start
  7.2 226.9 %reduce-scatter.3.cloned.1.call-start = ((), (), s32[]{:S(2)}) async-start(), calls=%async_computation.2 | async-start | bytes 786432 | tf_op jit(solution)/shard_map/reduce_scatter | solution.py:101
  9.1 3.0 copy-start.1
  9.2 5.9 %copy-start.2 = (s32[4,2]{0,1:T(2,128)S(1)}, s32[4,2]{0,1:T(2,128)}, u32[]{:S(2)}) copy-start(s32[4,2]{0,1:T(2,128)} %param.16) | copy-start | bytes 100
  9.5 93.6 %collective-permute-start = (bf16[2,1024,384]{2,1,0:T(8,128)(2,1)S(1)}, bf16[2,1024,384]{2,1,0:T(8,128)(2,1)}, u32[]{:S(2)}, u32[]{:S(2)}) collective-permute-start(bf16[2,1024,384]{2,1,0:T(8,128)(2,1)S(1)} %bitcast.145), channel_id=1, source_target_pairs={{2,0},{4,2},{6,4},{8,6},{10,8},{12,10},{14,12},{16,14},{18,16},{20... | collective-permute-start | bytes 4718600 | tf_op jit(solution)/shard_map/ppermute | solution.py:14
  10.8 92.3 %collective-permute-start.1 = (bf16[2,1024,384]{2,1,0:T(8,128)(2,1)S(1)}, bf16[2,1024,384]{2,1,0:T(8,128)(2,1)}, u32[]{:S(2)}, u32[]{:S(2)}) collective-permute-start(bf16[2,1024,384]{2,1,0:T(8,128)(2,1)S(1)} %bitcast.146), channel_id=1, source_target_pairs={{4,0},{6,2},{8,4},{10,6},{12,8},{14,10},{16,12},{18,14},{20,16},{2... | collective-permute-start | bytes 4718600 | tf_op jit(solution)/shard_map/ppermute | solution.py:14
  12.4 89.2 %collective-permute-start.2 = (bf16[2,1024,64]{2,1,0:T(8,128)(2,1)S(1)}, bf16[2,1024,64]{2,1,0:T(8,128)(2,1)S(1)}, u32[]{:S(2)}, u32[]{:S(2)}) collective-permute-start(bf16[2,1024,64]{2,1,0:T(8,128)(2,1)S(1)} %bitcast.150), channel_id=1, source_target_pairs={{2,0},{4,2},{6,4},{8,6},{10,8},{12,10},{14,12},{16,14},{18,16},{20... | collective-permute-start | bytes 786440 | tf_op jit(solution)/shard_map/ppermute | solution.py:14
  13.7 87.9 %collective-permute-start.3 = (bf16[2,1024,64]{2,1,0:T(8,128)(2,1)S(1)}, bf16[2,1024,64]{2,1,0:T(8,128)(2,1)S(1)}, u32[]{:S(2)}, u32[]{:S(2)}) collective-permute-start(bf16[2,1024,64]{2,1,0:T(8,128)(2,1)S(1)} %bitcast.151), channel_id=1, source_target_pairs={{4,0},{6,2},{8,4},{10,6},{12,8},{14,10},{16,12},{18,14},{20,16},{2... | collective-permute-start | bytes 786440 | tf_op jit(solution)/shard_map/ppermute | solution.py:14
  110.2 79.3 %collective-permute-start.4 = (f32[2,1024,64]{1,2,0:T(8,128)S(1)}, f32[2,1024,64]{1,2,0:T(8,128)S(1)}, u32[]{:S(2)}, u32[]{:S(2)}) collective-permute-start(f32[2,1024,64]{1,2,0:T(8,128)S(1)} %get-tuple-element.272), channel_id=1, source_target_pairs={{0,2},{2,4},{4,6},{6,8},{8,10},{10,12},{12,14},{14,16},{16,18},{18... | collective-permute-start | bytes 1572872 | tf_op jit(solution)/shard_map/ppermute | solution.py:14
  116.6 79.0 %collective-permute-start.5 = (f32[2,1024,64]{1,2,0:T(8,128)S(1)}, f32[2,1024,64]{1,2,0:T(8,128)S(1)}, u32[]{:S(2)}, u32[]{:S(2)}) collective-permute-start(f32[2,1024,64]{1,2,0:T(8,128)S(1)} %get-tuple-element.273), channel_id=1, source_target_pairs={{0,4},{2,6},{4,8},{6,10},{8,12},{10,14},{12,16},{14,18},{16,20},{1... | collective-permute-start | bytes 1572872 | tf_op jit(solution)/shard_map/ppermute | solution.py:14
  197.7 249.4 %reduce-scatter.5.cloned.1.call-start = ((), (), s32[]{:S(2)}) async-start(), calls=%async_computation.3 | async-start | bytes 786432 | tf_op jit(solution)/shard_map/reduce_scatter | solution.py:101
  329.4 24.9 %collective-permute-start.6 = (bf16[2,1024,64]{2,1,0:T(8,128)(2,1)S(1)}, bf16[2,1024,64]{2,1,0:T(8,128)(2,1)S(1)}, u32[]{:S(2)}, u32[]{:S(2)}) collective-permute-start(bf16[2,1024,64]{2,1,0:T(8,128)(2,1)S(1)} %bitcast.153), channel_id=1, source_target_pairs={{2,0},{4,2},{6,4},{8,6},{10,8},{12,10},{14,12},{16,14},{18,16},{20... | collective-permute-start | bytes 786440 | tf_op jit(solution)/shard_map/ppermute | solution.py:14
  330.7 23.6 %collective-permute-start.7 = (bf16[2,1024,64]{2,1,0:T(8,128)(2,1)S(1)}, bf16[2,1024,64]{2,1,0:T(8,128)(2,1)S(1)}, u32[]{:S(2)}, u32[]{:S(2)}) collective-permute-start(bf16[2,1024,64]{2,1,0:T(8,128)(2,1)S(1)} %bitcast.154), channel_id=1, source_target_pairs={{4,0},{6,2},{8,4},{10,6},{12,8},{14,10},{16,12},{18,14},{20,16},{2... | collective-permute-start | bytes 786440 | tf_op jit(solution)/shard_map/ppermute | solution.py:14
  359.1 48.8 %collective-permute-start.8 = (f32[2,1024,64]{1,2,0:T(8,128)S(1)}, f32[2,1024,64]{1,2,0:T(8,128)S(1)}, u32[]{:S(2)}, u32[]{:S(2)}) collective-permute-start(f32[2,1024,64]{1,2,0:T(8,128)S(1)} %get-tuple-element.270), channel_id=1, source_target_pairs={{0,2},{2,4},{4,6},{6,8},{8,10},{10,12},{12,14},{14,16},{16,18},{18... | collective-permute-start | bytes 1572872 | tf_op jit(solution)/shard_map/ppermute | solution.py:14
  362.7 56.6 %collective-permute-start.9 = (f32[2,1024,64]{1,2,0:T(8,128)S(1)}, f32[2,1024,64]{1,2,0:T(8,128)S(1)}, u32[]{:S(2)}, u32[]{:S(2)}) collective-permute-start(f32[2,1024,64]{1,2,0:T(8,128)S(1)} %get-tuple-element.271), channel_id=1, source_target_pairs={{0,4},{2,6},{4,8},{6,10},{8,12},{10,14},{12,16},{14,18},{16,20},{1... | collective-permute-start | bytes 1572872 | tf_op jit(solution)/shard_map/ppermute | solution.py:14
Sparse Core Ops, SparseCore 0:
  197.8 36.2 reduce-scatter.2
  421.4 25.5 reduce-scatter.4
where the time goes:
time: 550 us; the launch traced here: 548 us
  waiting for transfers between devices  188 us (34%)
  blocking collectives  158 us (29%)
  starting transfers between devices  136 us (25%)
  other arithmetic  36.2 us (7%)
  between operations  14.3 us (3%)
  local copies, waits for them, and re-layouts  8.38 us (2%)
  matrix products  6.27 us (1%)
    psum x2, blocking collectives, orthonormal(): gram_matrix = lax.psum(gram_matrix, ('rows', 'cols')) / rows_total  155 us
    ppermute x10, starting transfers between devices, shifted(): lax.ppermute(value, axis, [(source, source + steps) for source in range(i...  136 us
    ppermute x10, waiting for transfers between devices, shifted(): lax.ppermute(value, axis, [(source, source + steps) for source in range(i...  126 us
    reduce_scatter x2, waiting for transfers between devices, affinity_pass(): return lax.psum_scatter(flattened, 'cols', scatter_dimension=0, tiled=True)  62.1 us
    another operation x6, other arithmetic, orthonormal(): lower_factor = jnp.linalg.cholesky(gram_matrix)  13 us
  transfers between devices with their start and end apart: 12, of which 6 were waited for; matrix products, arithmetic and copies ran while one was open for 0% of the time, Pallas kernels for 0%

commit v1 on v0

--- a/solution.py
+++ b/solution.py
@@ -53,7 +53,7 @@
         precision=lax.Precision.HIGHEST,
         preferred_element_type=jnp.float32,
     )
-    gram_matrix = lax.psum(gram_matrix, ("rows", "cols")) / rows_total
+    gram_matrix = jnp.sum(lax.all_gather(gram_matrix, ("rows", "cols")), axis=0) / rows_total
     lower_factor = jnp.linalg.cholesky(gram_matrix)
     solved = lax.linalg.triangular_solve(
         lower_factor, sketch_rows, left_side=False, lower=True, transpose_a=True

time: 550 us -> 647 us (1.18)
  waiting for transfers between devices: 188 us -> 429 us
  blocking collectives: 158 us -> 1.99 us
  other arithmetic: 36.2 us -> 44.2 us
    all_gather x0 -> x2, waiting for transfers between devices: none -> 243 us  [orthonormal(): lax.all_gather(gram_matrix, ('rows', 'cols'))]
    psum x2 -> x0, blocking collectives: 155 us -> none  [orthonormal(): gram_matrix = lax.psum(gram_matrix, ('rows', 'cols')) / rows_total]
    reduce_sum x0 -> x2, other arithmetic: none -> 8.11 us  [orthonormal(): jnp.sum(lax.all_gather(gram_matrix, ('rows', 'cols')), axis=0) / rows_total]
  transfers between devices with their start and end apart: 12 -> 14, of which waited for: 6 -> 8; matrix products, arithmetic and copies ran while one was open for 0% -> 0% of each run, Pallas kernels for 0% -> 0%
where the time goes in v1:
time: 647 us; the launch traced here: 645 us
  waiting for transfers between devices  429 us (66%)
  starting transfers between devices  140 us (22%)
  other arithmetic  44.2 us (7%)
  between operations  14.1 us (2%)
  local copies, waits for them, and re-layouts  8.58 us (1%)
    all_gather x2, waiting for transfers between devices, orthonormal(): lax.all_gather(gram_matrix, ('rows', 'cols'))  243 us
    ppermute x10, starting transfers between devices, shifted(): lax.ppermute(value, axis, [(source, source + steps) for source in range(i...  140 us
    ppermute x10, waiting for transfers between devices, shifted(): lax.ppermute(value, axis, [(source, source + steps) for source in range(i...  124 us
    reduce_scatter x2, waiting for transfers between devices, affinity_pass(): return lax.psum_scatter(flattened, 'cols', scatter_dimension=0, tiled=True)  61.4 us
    another operation x6, other arithmetic, orthonormal(): lower_factor = jnp.linalg.cholesky(gram_matrix)  13 us
  transfers between devices with their start and end apart: 14, of which 8 were waited for; matrix products, arithmetic and copies ran while one was open for 0% of the time, Pallas kernels for 0%

profile of v1, /device:TPU:1, one launch (start us, length us, event | category | flops | bytes accessed | tf_op | source)
XLA Modules:
  0.0 644.7 jit_solution(16288063069667614076)
XLA Ops:
  7.2 1.9 fusion.32
  9.5 1.3 collective-permute-start
  10.8 1.3 collective-permute-start.1
  12.4 1.3 collective-permute-start.2
  13.7 1.3 collective-permute-start.3
  15.0 0.6 fusion.44
  15.7 85.9 %collective-permute-done.2 = bf16[2,1024,64]{2,1,0:T(8,128)(2,1)S(1)} collective-permute-done((bf16[2,1024,64]{2,1,0:T(8,128)(2,1)S(1)}, bf16[2,1024,64]{2,1,0:T(8,128)(2,1)S(1)}, u32[]{:S(2)}, u32[]{:S(2)}) %collective-permute-start.2) | collective-permute-done | bytes 262176 | tf_op jit(solution)/shard_map/ppermute | solution.py:14
  101.6 1.5 pad_maximum_fusion.1
  103.1 3.8 pad_maximum_fusion
  106.9 1.3 broadcast.76.clone
  108.2 0.7 while.24
  108.9 1.3 fusion.48
  110.2 6.4 collective-permute-start.4
  116.6 72.7 %collective-permute-start.5 = (f32[2,1024,64]{1,2,0:T(8,128)S(1)}, f32[2,1024,64]{1,2,0:T(8,128)S(1)}, u32[]{:S(2)}, u32[]{:S(2)}) collective-permute-start(f32[2,1024,64]{1,2,0:T(8,128)S(1)} %get-tuple-element.275), channel_id=1, source_target_pairs={{0,4},{2,6},{4,8},{6,10},{8,12},{10,14},{12,16},{14,18},{16,20},{1... | collective-permute-start | bytes 1572872 | tf_op jit(solution)/shard_map/ppermute | solution.py:14
  189.3 6.1 collective-permute-done.5
  195.4 1.1 add_bitcast_fusion.1
  196.5 0.9 copy.33
  197.4 36.4 %reduce-scatter.3.cloned.1.call-done = f32[1024,64]{0,1:T(8,128)} async-done(((f32[2048,64]{0,1:T(8,128)}), f32[1024,64]{0,1:T(8,128)}) %reduce-scatter.3.cloned.1.call-update) | async-done | bytes 262160 | tf_op jit(solution)/shard_map/reduce_scatter | solution.py:101
  233.8 2.0 fusion.49
  235.9 122.1 %all-gather.5.cloned.1.call-done = f32[16384,64]{1,0:T(8,128)} async-done(((f32[64,64]{1,0:T(8,128)}), f32[16384,64]{1,0:T(8,128)}) %all-gather.5.cloned.1.call-update) | async-done | bytes 4194320 | tf_op jit(solution)/shard_map/all_gather | solution.py:56
  358.0 4.1 reduce_sum.42
  362.2 5.8 cholesky.44
  368.1 0.6 compare_reduce_fusion.1
  368.7 0.7 fusion.35
  369.4 4.9 custom-call.6
  374.7 2.0 all_gather.17
  377.0 1.3 collective-permute-start.6
  378.3 1.3 collective-permute-start.7
  379.6 20.4 %collective-permute-done.6 = bf16[2,1024,64]{2,1,0:T(8,128)(2,1)S(1)} collective-permute-done((bf16[2,1024,64]{2,1,0:T(8,128)(2,1)S(1)}, bf16[2,1024,64]{2,1,0:T(8,128)(2,1)S(1)}, u32[]{:S(2)}, u32[]{:S(2)}) %collective-permute-start.6) | collective-permute-done | bytes 262176 | tf_op jit(solution)/shard_map/ppermute | solution.py:14
  400.0 1.5 pad_maximum_fusion.2
  401.5 1.3 broadcast.76
  402.8 0.7 while.25
  403.5 1.3 fusion.47
  404.8 7.5 %collective-permute-start.8 = (f32[2,1024,64]{1,2,0:T(8,128)S(1)}, f32[2,1024,64]{1,2,0:T(8,128)S(1)}, u32[]{:S(2)}, u32[]{:S(2)}) collective-permute-start(f32[2,1024,64]{1,2,0:T(8,128)S(1)} %get-tuple-element.272), channel_id=1, source_target_pairs={{0,2},{2,4},{4,6},{6,8},{8,10},{10,12},{12,14},{14,16},{16,18},{18... | collective-permute-start | bytes 1572872 | tf_op jit(solution)/shard_map/ppermute | solution.py:14
  412.3 45.2 %collective-permute-start.9 = (f32[2,1024,64]{1,2,0:T(8,128)S(1)}, f32[2,1024,64]{1,2,0:T(8,128)S(1)}, u32[]{:S(2)}, u32[]{:S(2)}) collective-permute-start(f32[2,1024,64]{1,2,0:T(8,128)S(1)} %get-tuple-element.273), channel_id=1, source_target_pairs={{0,4},{2,6},{4,8},{6,10},{8,12},{10,14},{12,16},{14,18},{16,20},{1... | collective-permute-start | bytes 1572872 | tf_op jit(solution)/shard_map/ppermute | solution.py:14
  457.5 11.8 %collective-permute-done.9 = f32[2,1024,64]{1,2,0:T(8,128)S(1)} collective-permute-done((f32[2,1024,64]{1,2,0:T(8,128)S(1)}, f32[2,1024,64]{1,2,0:T(8,128)S(1)}, u32[]{:S(2)}, u32[]{:S(2)}) %collective-permute-start.9) | collective-permute-done | bytes 524320 | tf_op jit(solution)/shard_map/ppermute | solution.py:14
  469.3 1.1 add_bitcast_fusion
  470.5 0.9 copy.34
  471.6 25.0 %reduce-scatter.5.cloned.1.call-done = f32[1024,64]{0,1:T(8,128)} async-done(((f32[2048,64]{0,1:T(8,128)}), f32[1024,64]{0,1:T(8,128)}) %reduce-scatter.5.cloned.1.call-update) | async-done | bytes 262160 | tf_op jit(solution)/shard_map/reduce_scatter | solution.py:101
  496.6 2.0 fusion.50
  498.6 121.4 %all-gather.7.cloned.1.call-done = f32[16384,64]{1,0:T(8,128)} async-done(((f32[64,64]{1,0:T(8,128)}), f32[16384,64]{1,0:T(8,128)}) %all-gather.7.cloned.1.call-update) | async-done | bytes 4194320 | tf_op jit(solution)/shard_map/all_gather | solution.py:56
  620.0 4.1 reduce_sum.43
  624.3 5.8 cholesky.55
  630.1 0.6 compare_reduce_fusion
  630.8 0.7 fusion.43
  631.4 4.9 custom-call.7
  636.3 0.7 copy.31
  637.1 1.1 convolution_bitcast_fusion.2
  (39 shorter events, 2.2 us)
Async XLA Ops:
  7.2 2.0 copy-start
  7.2 226.6 %reduce-scatter.3.cloned.1.call-start = ((), (), s32[]{:S(2)}) async-start(), calls=%async_computation.2 | async-start | bytes 786432 | tf_op jit(solution)/shard_map/reduce_scatter | solution.py:101
  9.1 3.0 copy-start.3
  9.2 5.9 copy-start.4
  9.5 93.6 %collective-permute-start = (bf16[2,1024,384]{2,1,0:T(8,128)(2,1)S(1)}, bf16[2,1024,384]{2,1,0:T(8,128)(2,1)}, u32[]{:S(2)}, u32[]{:S(2)}) collective-permute-start(bf16[2,1024,384]{2,1,0:T(8,128)(2,1)S(1)} %bitcast.149), channel_id=1, source_target_pairs={{2,0},{4,2},{6,4},{8,6},{10,8},{12,10},{14,12},{16,14},{18,16},{20... | collective-permute-start | bytes 4718600 | tf_op jit(solution)/shard_map/ppermute | solution.py:14
  10.8 92.3 %collective-permute-start.1 = (bf16[2,1024,384]{2,1,0:T(8,128)(2,1)S(1)}, bf16[2,1024,384]{2,1,0:T(8,128)(2,1)}, u32[]{:S(2)}, u32[]{:S(2)}) collective-permute-start(bf16[2,1024,384]{2,1,0:T(8,128)(2,1)S(1)} %bitcast.150), channel_id=1, source_target_pairs={{4,0},{6,2},{8,4},{10,6},{12,8},{14,10},{16,12},{18,14},{20,16},{2... | collective-permute-start | bytes 4718600 | tf_op jit(solution)/shard_map/ppermute | solution.py:14
  12.4 89.2 %collective-permute-start.2 = (bf16[2,1024,64]{2,1,0:T(8,128)(2,1)S(1)}, bf16[2,1024,64]{2,1,0:T(8,128)(2,1)S(1)}, u32[]{:S(2)}, u32[]{:S(2)}) collective-permute-start(bf16[2,1024,64]{2,1,0:T(8,128)(2,1)S(1)} %bitcast.154), channel_id=1, source_target_pairs={{2,0},{4,2},{6,4},{8,6},{10,8},{12,10},{14,12},{16,14},{18,16},{20... | collective-permute-start | bytes 786440 | tf_op jit(solution)/shard_map/ppermute | solution.py:14
  13.7 87.9 %collective-permute-start.3 = (bf16[2,1024,64]{2,1,0:T(8,128)(2,1)S(1)}, bf16[2,1024,64]{2,1,0:T(8,128)(2,1)S(1)}, u32[]{:S(2)}, u32[]{:S(2)}) collective-permute-start(bf16[2,1024,64]{2,1,0:T(8,128)(2,1)S(1)} %bitcast.155), channel_id=1, source_target_pairs={{4,0},{6,2},{8,4},{10,6},{12,8},{14,10},{16,12},{18,14},{20,16},{2... | collective-permute-start | bytes 786440 | tf_op jit(solution)/shard_map/ppermute | solution.py:14
  110.2 79.1 %collective-permute-start.4 = (f32[2,1024,64]{1,2,0:T(8,128)S(1)}, f32[2,1024,64]{1,2,0:T(8,128)S(1)}, u32[]{:S(2)}, u32[]{:S(2)}) collective-permute-start(f32[2,1024,64]{1,2,0:T(8,128)S(1)} %get-tuple-element.274), channel_id=1, source_target_pairs={{0,2},{2,4},{4,6},{6,8},{8,10},{10,12},{12,14},{14,16},{16,18},{18... | collective-permute-start | bytes 1572872 | tf_op jit(solution)/shard_map/ppermute | solution.py:14
  116.6 78.8 %collective-permute-start.5 = (f32[2,1024,64]{1,2,0:T(8,128)S(1)}, f32[2,1024,64]{1,2,0:T(8,128)S(1)}, u32[]{:S(2)}, u32[]{:S(2)}) collective-permute-start(f32[2,1024,64]{1,2,0:T(8,128)S(1)} %get-tuple-element.275), channel_id=1, source_target_pairs={{0,4},{2,6},{4,8},{6,10},{8,12},{10,14},{12,16},{14,18},{16,20},{1... | collective-permute-start | bytes 1572872 | tf_op jit(solution)/shard_map/ppermute | solution.py:14
  197.4 160.6 %all-gather.5.cloned.1.call-start = ((), (), s32[]{:S(2)}) async-start(), calls=%async_computation.4 | async-start | bytes 8421376 | tf_op jit(solution)/shard_map/all_gather | solution.py:56
  235.8 260.8 %reduce-scatter.5.cloned.1.call-start = ((), (), s32[]{:S(2)}) async-start(), calls=%async_computation.3 | async-start | bytes 786432 | tf_op jit(solution)/shard_map/reduce_scatter | solution.py:101
  358.0 16.3 %copy-start.2 = (f32[1024,64]{0,1:T(8,128)S(1)}, f32[1024,64]{0,1:T(8,128)}, u32[]{:S(2)}) copy-start(f32[1024,64]{0,1:T(8,128)} %reduce-scatter.3.cloned.1.call-done) | copy-start | bytes 786436
  377.0 23.0 %collective-permute-start.6 = (bf16[2,1024,64]{2,1,0:T(8,128)(2,1)S(1)}, bf16[2,1024,64]{2,1,0:T(8,128)(2,1)S(1)}, u32[]{:S(2)}, u32[]{:S(2)}) collective-permute-start(bf16[2,1024,64]{2,1,0:T(8,128)(2,1)S(1)} %bitcast.157), channel_id=1, source_target_pairs={{2,0},{4,2},{6,4},{8,6},{10,8},{12,10},{14,12},{16,14},{18,16},{20... | collective-permute-start | bytes 786440 | tf_op jit(solution)/shard_map/ppermute | solution.py:14
  378.3 21.7 %collective-permute-start.7 = (bf16[2,1024,64]{2,1,0:T(8,128)(2,1)S(1)}, bf16[2,1024,64]{2,1,0:T(8,128)(2,1)S(1)}, u32[]{:S(2)}, u32[]{:S(2)}) collective-permute-start(bf16[2,1024,64]{2,1,0:T(8,128)(2,1)S(1)} %bitcast.158), channel_id=1, source_target_pairs={{4,0},{6,2},{8,4},{10,6},{12,8},{14,10},{16,12},{18,14},{20,16},{2... | collective-permute-start | bytes 786440 | tf_op jit(solution)/shard_map/ppermute | solution.py:14
  404.8 52.8 %collective-permute-start.8 = (f32[2,1024,64]{1,2,0:T(8,128)S(1)}, f32[2,1024,64]{1,2,0:T(8,128)S(1)}, u32[]{:S(2)}, u32[]{:S(2)}) collective-permute-start(f32[2,1024,64]{1,2,0:T(8,128)S(1)} %get-tuple-element.272), channel_id=1, source_target_pairs={{0,2},{2,4},{4,6},{6,8},{8,10},{10,12},{12,14},{14,16},{16,18},{18... | collective-permute-start | bytes 1572872 | tf_op jit(solution)/shard_map/ppermute | solution.py:14
  412.3 57.1 %collective-permute-start.9 = (f32[2,1024,64]{1,2,0:T(8,128)S(1)}, f32[2,1024,64]{1,2,0:T(8,128)S(1)}, u32[]{:S(2)}, u32[]{:S(2)}) collective-permute-start(f32[2,1024,64]{1,2,0:T(8,128)S(1)} %get-tuple-element.273), channel_id=1, source_target_pairs={{0,4},{2,6},{4,8},{6,10},{8,12},{10,14},{12,16},{14,18},{16,20},{1... | collective-permute-start | bytes 1572872 | tf_op jit(solution)/shard_map/ppermute | solution.py:14
  471.3 148.7 %all-gather.7.cloned.1.call-start = ((), (), s32[]{:S(2)}) async-start(), calls=%async_computation.5 | async-start | bytes 8421376 | tf_op jit(solution)/shard_map/all_gather | solution.py:56
  620.0 17.0 %copy-start.1 = (f32[1024,64]{0,1:T(8,128)S(1)}, f32[1024,64]{0,1:T(8,128)}, u32[]{:S(2)}) copy-start(f32[1024,64]{0,1:T(8,128)} %reduce-scatter.5.cloned.1.call-done) | copy-start | bytes 786436
Sparse Core Ops, SparseCore 0:
  197.5 36.2 reduce-scatter.2
  238.7 119.2 all-gather.4
  471.5 25.0 reduce-scatter.4
  500.7 119.2 all-gather.6
